TPU v7x, 32 devices: a whole 2x2x4 slice. The times are simulated.
32 devices in a mesh: grp: 4 (over x, core), dp: 4 (over z), seq: 2 (over y).
Axes of the slice: x: 2, y: 2, z: 4, core: 2. Of those that a mesh axis runs over, the one named last changes fastest.
Arguments:
- student_saved_input: bfloat16 [16, 256, 3584], P(('grp', 'dp'), 'seq'), may hold values from -6 to 6
- student_saved_query: bfloat16 [16, 256, 1792], P(('grp', 'dp'), 'seq'), may hold values from -600 to 600
- feature_cotangent: bfloat16 [16, 256, 1792], P(('grp', 'dp'), 'seq'), may hold values from -6 to 6
- feature_weights: bfloat16 [128, 896], replicated, may hold values from -0.5 to 0.5
- adapter_down_weight: bfloat16 [8, 3584], replicated, may hold values from -0.09375 to 0.09375
- adapter_up_weight: bfloat16 [8, 1792], replicated, may hold values from -0.09375 to 0.09375
- teacher_next_query: bfloat16 [16, 512, 1792], P(('grp', 'dp'), 'seq'), may hold values from -6 to 6
- teacher_next_key: bfloat16 [16, 512, 256], P(('grp', 'dp'), 'seq'), may hold values from -6 to 6
- teacher_next_value: bfloat16 [16, 512, 256], P(('grp', 'dp'), 'seq'), may hold values from -6 to 6
- positions: int32 [16, 512], P(('grp', 'dp'), 'seq'), may hold values from 0 to 511, each once within a row
Outputs:
- teacher_output: bfloat16 [16, 512, 1792], P(('grp', 'dp'), 'seq')
- grad_feature: float32 [128, 896], P('dp')
- grad_down: float32 [8, 3584], P(None, 'dp')
- up_gradient: float32 [8, 1792], P(None, 'dp')
Inputs may be any that keep to these rules, and one draw needn't show every extreme that they name: `positions`: each sequence's row is a permutation of 0 to 511.
All inputs are finite; a program needn't handle non-finite values.
Results may differ from a plain program's by a relative error of at most 0.015.
Values may be sent and summed in bfloat16 or wider, within the bound.
No kernel may reach another device: no remote copies, remote signals or barrier semaphores. Data moves between devices by JAX's collectives and lax.ppermute only.
A program may use at most 64 MiB of HBM per device.

v0:
```python
import jax
import jax.numpy as jnp
from jax import lax
from jax.sharding import PartitionSpec as P

HEAD_SIZE = 128
F = 64


adapter_scale = 2.0
masked_score = -1e30
key_block = 512


def student_gradients(
    student_saved_input,
    student_saved_query,
    feature_cotangent,
    feature_weights,
    adapter_down_weight,
    adapter_up_weight,
):
    row_count = student_saved_query.shape[0] * student_saved_query.shape[1]
    head_count = feature_weights.shape[1] // F
    heads_of_queries = student_saved_query.reshape(row_count, head_count, HEAD_SIZE)
    map_heads = feature_weights.reshape(HEAD_SIZE, head_count, F)
    logits = jnp.einsum(
        "shd,dhf->shf", heads_of_queries, map_heads, preferred_element_type=jnp.float32
    )
    prob_plus = jax.nn.softmax(logits, axis=-1)
    prob_minus = jax.nn.softmax(-logits, axis=-1)
    cotangent = feature_cotangent.reshape(row_count, head_count, 2 * F).astype(jnp.float32)
    cot_plus = cotangent[..., :F]
    cot_minus = cotangent[..., F:]
    dlogit = prob_plus * (
        cot_plus - jnp.sum(prob_plus * cot_plus, axis=-1, keepdims=True)
    ) - prob_minus * (cot_minus - jnp.sum(prob_minus * cot_minus, axis=-1, keepdims=True))
    dlogit_b = dlogit.astype(jnp.bfloat16)
    grad_map = jnp.einsum(
        "shd,shf->dhf", heads_of_queries, dlogit_b, preferred_element_type=jnp.float32
    ).reshape(HEAD_SIZE, head_count * F)
    query_gradient = (
        jnp.einsum("shf,dhf->shd", dlogit_b, map_heads, preferred_element_type=jnp.float32)
        .reshape(row_count, head_count * HEAD_SIZE)
        .astype(jnp.bfloat16)
    )
    input_rows = student_saved_input.reshape(row_count, -1)
    down_activation = jnp.dot(
        input_rows, adapter_down_weight.T, preferred_element_type=jnp.float32
    ).astype(jnp.bfloat16)
    up_gradient = adapter_scale * jnp.dot(
        down_activation.T, query_gradient, preferred_element_type=jnp.float32
    )
    lowrank_gradient = (
        adapter_scale
        * jnp.dot(query_gradient, adapter_up_weight.T, preferred_element_type=jnp.float32)
    ).astype(jnp.bfloat16)
    grad_down = jnp.dot(lowrank_gradient.T, input_rows, preferred_element_type=jnp.float32)
    return (grad_map, grad_down, up_gradient)


def reduce_grads(grads):
    along_seq = (
        lax.psum(grads[0].astype(jnp.bfloat16), "seq").astype(jnp.float32),
        lax.psum(grads[1].astype(jnp.bfloat16), "seq").astype(jnp.float32),
        lax.psum(grads[2].astype(jnp.bfloat16), "seq").astype(jnp.float32),
    )
    shards = (
        lax.psum_scatter(
            along_seq[0].astype(jnp.bfloat16), "dp", scatter_dimension=0, tiled=True
        ).astype(jnp.float32),
        lax.psum_scatter(
            along_seq[1].astype(jnp.bfloat16), "dp", scatter_dimension=1, tiled=True
        ).astype(jnp.float32),
        lax.psum_scatter(
            along_seq[2].astype(jnp.bfloat16), "dp", scatter_dimension=1, tiled=True
        ).astype(jnp.float32),
    )
    return (
        lax.psum(shards[0].astype(jnp.bfloat16), "grp").astype(jnp.float32),
        lax.psum(shards[1].astype(jnp.bfloat16), "grp").astype(jnp.float32),
        lax.psum(shards[2].astype(jnp.bfloat16), "grp").astype(jnp.float32),
    )


def teacher_attention(teacher_next_query, teacher_next_key, teacher_next_value, positions):
    query_count = teacher_next_query.shape[1]
    kv_heads = teacher_next_key.shape[2] // HEAD_SIZE
    group_width = teacher_next_query.shape[2] // HEAD_SIZE // kv_heads
    heads_of_queries = teacher_next_query[0].reshape(query_count, kv_heads, group_width, HEAD_SIZE)
    query_pos = positions[0]
    scale_factor = HEAD_SIZE ** (-0.5)

    def one_block(state, rows_of_keys, rows_of_values, key_pos):
        running_max, denom, accum = state
        score = (
            jnp.einsum(
                "qcgd,kcd->cgqk", heads_of_queries, rows_of_keys, preferred_element_type=jnp.float32
            )
            * scale_factor
        )
        allowed = (key_pos[None, :] <= query_pos[:, None])[None, None]
        score = jnp.where(allowed, score, masked_score)
        new_max = jnp.maximum(running_max, jnp.max(score, axis=-1))
        factor = jnp.exp(running_max - new_max)
        weights = jnp.where(allowed, jnp.exp(score - new_max[..., None]), 0.0)
        denom = denom * factor + jnp.sum(weights, axis=-1)
        update = jnp.einsum(
            "cgqk,kcd->qcgd",
            weights.astype(jnp.bfloat16),
            rows_of_values,
            preferred_element_type=jnp.float32,
        )
        accum = accum * jnp.transpose(factor, (2, 0, 1))[..., None] + update
        return (new_max, denom, accum)

    start_state = (
        jnp.full((kv_heads, group_width, query_count), masked_score, jnp.float32),
        jnp.zeros((kv_heads, group_width, query_count), jnp.float32),
        jnp.zeros((query_count, kv_heads, group_width, HEAD_SIZE), jnp.float32),
    )
    key_piece = lax.all_gather(teacher_next_key, "seq", axis=1, tiled=True)
    value_piece = lax.all_gather(teacher_next_value, "seq", axis=1, tiled=True)
    pos_piece = lax.all_gather(positions, "seq", axis=1, tiled=True)
    piece_rows = key_piece.shape[1]
    keys_all = key_piece[0].reshape(piece_rows, kv_heads, HEAD_SIZE)
    values_all = value_piece[0].reshape(piece_rows, kv_heads, HEAD_SIZE)
    pos_all = pos_piece[0]

    def advance(index, inner):
        begin = index * key_block
        return one_block(
            inner,
            lax.dynamic_slice_in_dim(keys_all, begin, key_block, 0),
            lax.dynamic_slice_in_dim(values_all, begin, key_block, 0),
            lax.dynamic_slice_in_dim(pos_all, begin, key_block, 0),
        )

    running_max, denom, accum = lax.fori_loop(0, piece_rows // key_block, advance, start_state)
    output = accum / jnp.transpose(denom, (2, 0, 1))[..., None]
    return output.astype(jnp.bfloat16).reshape(1, query_count, -1)


def on_device(
    student_saved_input,
    student_saved_query,
    feature_cotangent,
    feature_weights,
    adapter_down_weight,
    adapter_up_weight,
    teacher_next_query,
    teacher_next_key,
    teacher_next_value,
    positions,
):
    teacher_output = teacher_attention(
        teacher_next_query, teacher_next_key, teacher_next_value, positions
    )
    grads = student_gradients(
        student_saved_input,
        student_saved_query,
        feature_cotangent,
        feature_weights,
        adapter_down_weight,
        adapter_up_weight,
    )
    grad_feature, grad_down, up_gradient = reduce_grads(grads)
    return (teacher_output, grad_feature, grad_down, up_gradient)


def solution(mesh):
    placed = (
        P(("grp", "dp"), "seq", None),
        P(("grp", "dp"), "seq", None),
        P(("grp", "dp"), "seq", None),
        P(),
        P(),
        P(),
        P(("grp", "dp"), "seq", None),
        P(("grp", "dp"), "seq", None),
        P(("grp", "dp"), "seq", None),
        P(("grp", "dp"), "seq"),
    )
    return jax.shard_map(
        on_device,
        mesh=mesh,
        in_specs=placed,
        out_specs=(P(("grp", "dp"), "seq", None), P("dp", None), P(None, "dp"), P(None, "dp")),
        check_vma=False,
    )
```

profile of v0, /device:TPU:0, one launch (start us, length us, event | category | flops | bytes accessed | tf_op | source)
XLA Modules:
  0.0 152.9 jit_solution(6718897974709875448)
XLA Ops:
  7.2 0.0 copy-start
  7.2 0.0 copy-start.4
  7.2 0.0 copy-start.5
  7.2 0.0 reduce-scatter.12.cloned.1.call-start
  7.2 1.3 copy.44
  8.6 1.1 copy.43
  9.7 0.3 fusion.20
  10.0 0.0 copy-start.6
  10.0 1.1 fusion.18
  11.1 1.2 copy.46
  12.3 0.5 fusion.27
  12.8 1.5 convolution_convert_fusion.1
  14.3 0.0 copy-start.3
  14.4 0.0 copy-done
  14.4 0.0 copy-done.4
  14.4 0.8 fusion.12
  15.2 1.0 copy.60
  16.1 0.0 reduce-scatter.12.cloned.1.call-update
  16.2 0.0 reduce-scatter.10.cloned.1.call-start
  16.2 0.0 copy-done.5
  16.2 0.4 convolution_convert_fusion
  16.6 1.3 copy.58
  17.9 0.0 reduce-scatter.10.cloned.1.call-update
  17.9 0.0 reduce-scatter.8.cloned.1.call-start
  17.9 1.6 %convolution_convert_fusion.2 = bf16[14,64,128]{2,1,0:T(8,128)(2,1)S(1)} fusion(bf16[128,14,128]{0,2,1:T(8,128)(2,1)S(1)} %bitcast.93, f32[128,14,64]{0,2,1:T(8,128)S(1)} %fusion.27, f32[128,14,64]{0,2,1:T(8,128)} %fusion.18, f32[128,14,128]{0,2,1:T(8,128)S(1)} %bitcast.89), kind=kOutput, calls=%fused_computation.33 | convolution fusion | flops 30050112 | bytes 2981888 | tf_op jit(solution)/shard_map/shd,shf->dhf/dot_general | solution.py:39
  19.5 0.8 copy.48
  20.4 0.0 reduce-scatter.8.cloned.1.call-update
  20.4 0.0 all-reduce.7.cloned.1.call-start
  20.4 0.0 copy-done.6
  20.4 5.2 %all_gather.11 = s32[1,512]{1,0:T(1,128)S(1)} all-gather(s32[1,256]{1,0:T(1,128)S(1)} %copy-done.6), channel_id=1, replica_groups=mesh['grp'=4,'dp'=4,'seq'=2] {'seq'}, dimensions={1}, use_global_device_ids=true | all-gather | bytes 3072 | tf_op jit(solution)/shard_map/all_gather | solution.py:124
  25.6 1.5 copy.38
  27.1 0.0 copy-done.3
  27.1 0.1 copy.37
  27.2 5.6 %all_gather.13 = bf16[1,512,256]{1,2,0:T(8,128)(2,1)S(1)} all-gather(bf16[1,256,256]{1,2,0:T(8,128)(2,1)S(1)} %copy.37), channel_id=1, replica_groups=mesh['grp'=4,'dp'=4,'seq'=2] {'seq'}, dimensions={1}, use_global_device_ids=true | all-gather | bytes 393216 | tf_op jit(solution)/shard_map/all_gather | solution.py:122
  32.9 0.1 broadcast_compare_fusion
  33.0 0.0 copy-start.2
  33.0 1.3 fusion.6
  34.4 0.0 copy-start.1
  34.4 2.9 %copy-done.1 = f32[2,512,256,7]{2,1,3,0:T(8,128)} copy-done((f32[2,512,256,7]{2,1,3,0:T(8,128)}, f32[2,512,256,7]{2,1,3,0:T(8,128)S(1)}, u32[]{:S(2)}) %copy-start.1) | copy-done | bytes 7340056
  37.3 1.8 %fusion.7 = f32[2,7,256]{2,1,0:T(8,128)S(1)} fusion(f32[2,512,256,7]{2,1,3,0:T(8,128)S(1)} %get-tuple-element.55, f32[2,7,256]{2,1,0:T(8,128)S(1)} %get-tuple-element.53, pred[256,512]{0,1:T(8,128)(4,1)S(1)} %broadcast_compare_fusion), kind=kLoop, calls=%fused_computation.9 | loop fusion | flops 9171456 | bytes 7499776 | tf_op jit(solution)/shard_map/while/body/eval_jaxpr/reduce_sum | solution.py:107
  39.2 1.2 reduce-scatter.12.cloned.1.call-done
  40.4 1.6 %copy.61 = bf16[8,448]{1,0:T(8,128)(2,1)} copy(bf16[8,448]{0,1:T(8,128)(2,1)} %bitcast.102) | data formatting | bytes 14336
  42.0 24.8 %reduce-scatter.10.cloned.1.call-done = bf16[896,8]{1,0:T(8,128)(2,1)} async-done(((bf16[3584,8]{1,0:T(8,128)(2,1)}), bf16[896,8]{1,0:T(8,128)(2,1)}) %reduce-scatter.10.cloned.1.call-update) | async-done | bytes 14352
  66.7 1.6 %copy.59 = bf16[8,896]{1,0:T(8,128)(2,1)} copy(bf16[8,896]{0,1:T(8,128)(2,1)} %bitcast.101) | data formatting | bytes 28672
  68.4 19.4 %reduce-scatter.8.cloned.1.call-done = bf16[32,896]{1,0:T(8,128)(2,1)} async-done(((bf16[128,896]{1,0:T(8,128)(2,1)}), bf16[32,896]{1,0:T(8,128)(2,1)}) %reduce-scatter.8.cloned.1.call-update) | async-done | bytes 57360 | tf_op jit(solution)/shard_map/reduce_scatter | solution.py:69
  87.7 0.0 all-reduce.7.cloned.1.call-update
  87.8 0.0 all-reduce.5.cloned.1.call-start
  87.8 0.0 copy-done.2
  87.9 5.6 %all_gather.14 = bf16[1,512,256]{2,1,0:T(8,128)(2,1)S(1)} all-gather(bf16[1,256,256]{2,1,0:T(8,128)(2,1)S(1)} %copy-done.2), channel_id=1, replica_groups=mesh['grp'=4,'dp'=4,'seq'=2] {'seq'}, dimensions={1}, use_global_device_ids=true | all-gather | bytes 393216 | tf_op jit(solution)/shard_map/all_gather | solution.py:123
  93.5 0.1 copy.41
  93.6 16.4 %all-reduce.7.cloned.1.call-done = (bf16[32,896]{1,0:T(8,128)(2,1)}, bf16[8,896]{1,0:T(8,128)(2,1)}, bf16[8,448]{1,0:T(8,128)(2,1)}) async-done(((bf16[32,896]{1,0:T(8,128)(2,1)}, bf16[8,896]{1,0:T(8,128)(2,1)}, bf16[8,448]{1,0:T(8,128)(2,1)}), (bf16[32,896]{1,0:T(8,128)(2,1)}, bf16[8,896]{1,0:T(8,128)(2,1)}, bf16[8,448]{1,0:T(8,128)(2,1)})) %all-reduce.7.cloned.1.call-update) | async-done | bytes 78864 | tf_op jit(solution)/shard_map/psum | solution.py:64
  110.1 0.0 all-reduce.5.cloned.1.call-update
  110.1 5.2 %fusion.14 = bf16[256,2,7,128]{0,3,2,1:T(8,128)(2,1)S(1)} fusion(bf16[512,2,128,1]{0,2,3,1:T(8,128)(2,1)S(1)} %bitcast.100, f32[2,512,256,7]{2,1,3,0:T(8,128)} %copy-done.1, f32[2,7,256]{2,1,0:T(8,128)S(1)} %get-tuple-element.53, pred[256,512]{0,1:T(8,128)(4,1)S(1)} %broadcast_compare_fusion, f32[256,2,7]{0,2,1:T(8,128)S(1)} %bitcast_add_fusion.1, ...), kind=kOutput, calls=%fused_computation.18 | convolution fusion | flops 480313344 | bytes 8693760 | tf_op jit(solution)/shard_map/while/body/eval_jaxpr/cgqk,kcd->qcgd/dot_general | solution.py:108
  115.3 1.4 copy.49
  116.6 25.7 %all-reduce.5.cloned.1.call-done = (bf16[32,896]{1,0:T(8,128)(2,1)}, bf16[8,896]{1,0:T(8,128)(2,1)}, bf16[8,448]{1,0:T(8,128)(2,1)}) async-done(((bf16[32,896]{1,0:T(8,128)(2,1)}, bf16[8,896]{1,0:T(8,128)(2,1)}, bf16[8,448]{1,0:T(8,128)(2,1)}), (bf16[32,896]{1,0:T(8,128)(2,1)}, bf16[8,896]{1,0:T(8,128)(2,1)}, bf16[8,448]{1,0:T(8,128)(2,1)})) %all-reduce.5.cloned.1.call-update) | async-done | bytes 78864 | tf_op jit(solution)/shard_map/psum | solution.py:80
  142.3 1.5 convert_element_type.75
  143.8 1.3 convert_element_type.81
  145.1 1.3 convert_element_type.84
  (2 shorter events, 0.0 us)
Async XLA Ops:
  7.2 7.2 %copy-start = (bf16[1,128,3584]{2,1,0:T(8,128)(2,1)S(1)}, bf16[1,128,3584]{2,1,0:T(8,128)(2,1)}, u32[]{:S(2)}) copy-start(bf16[1,128,3584]{2,1,0:T(8,128)(2,1)} %param.10) | copy-start | bytes 2752516
  7.2 7.2 %copy-start.4 = (bf16[8,3584]{1,0:T(8,128)(2,1)S(1)}, bf16[8,3584]{1,0:T(8,128)(2,1)}, u32[]{:S(2)}) copy-start(bf16[8,3584]{1,0:T(8,128)(2,1)} %param.14) | copy-start | bytes 172036
  7.2 9.0 %copy-start.5 = (bf16[8,1792]{1,0:T(8,128)(2,1)S(1)}, bf16[8,1792]{1,0:T(8,128)(2,1)}, u32[]{:S(2)}) copy-start(bf16[8,1792]{1,0:T(8,128)(2,1)} %param.15) | copy-start | bytes 86020
  7.2 33.2 %reduce-scatter.12.cloned.1.call-start = ((), (), s32[]{:S(2)}) async-start(), calls=%async_computation.5 | async-start | bytes 573440
  10.0 10.4 %copy-start.6 = (s32[1,256]{1,0:T(1,128)S(1)}, s32[1,256]{1,0:T(1,128)}, u32[]{:S(2)}) copy-start(s32[1,256]{1,0:T(1,128)} %param.19) | copy-start | bytes 3076
  14.3 12.8 %copy-start.3 = (bf16[1,256,256]{2,1,0:T(8,128)(2,1)S(1)}, bf16[1,256,256]{2,1,0:T(8,128)(2,1)}, u32[]{:S(2)}) copy-start(bf16[1,256,256]{2,1,0:T(8,128)(2,1)} %param.17) | copy-start | bytes 393220
  16.2 50.6 %reduce-scatter.10.cloned.1.call-start = ((), (), s32[]{:S(2)}) async-start(), calls=%async_computation.4 | async-start | bytes 1146880
  17.9 69.9 %reduce-scatter.8.cloned.1.call-start = ((), (), s32[]{:S(2)}) async-start(), calls=%async_computation.3 | async-start | bytes 286720 | tf_op jit(solution)/shard_map/reduce_scatter | solution.py:69
  20.4 89.7 %all-reduce.7.cloned.1.call-start = ((), (), s32[]{:S(2)}) async-start(), calls=%async_computation.7 | async-start | bytes 159744 | tf_op jit(solution)/shard_map/psum | solution.py:64
  33.0 54.8 %copy-start.2 = (bf16[1,256,256]{2,1,0:T(8,128)(2,1)S(1)}, bf16[1,256,256]{2,1,0:T(8,128)(2,1)}, u32[]{:S(2)}) copy-start(bf16[1,256,256]{2,1,0:T(8,128)(2,1)} %param.18) | copy-start | bytes 393220
  34.4 3.0 %copy-start.1 = (f32[2,512,256,7]{2,1,3,0:T(8,128)}, f32[2,512,256,7]{2,1,3,0:T(8,128)S(1)}, u32[]{:S(2)}) copy-start(f32[2,512,256,7]{2,1,3,0:T(8,128)S(1)} %get-tuple-element.55) | copy-start | bytes 22020100
  87.8 54.5 %all-reduce.5.cloned.1.call-start = ((), (), s32[]{:S(2)}) async-start(), calls=%async_computation.6 | async-start | bytes 159744 | tf_op jit(solution)/shard_map/psum | solution.py:80
Sparse Core Ops, SparseCore 0:
  16.3 24.0 reduce-scatter.11
  43.3 23.4 reduce-scatter.9
  69.0 18.6 reduce-scatter.7
  90.6 19.4 all-reduce.6
  112.4 29.8 all-reduce.4
where the time goes:
time: 153 us
  waiting for transfers between devices  87.6 us (57%)
  blocking collectives  16.5 us (11%)
  local copies, waits for them, and re-layouts  16 us (10%)
  between operations  14 us (9%)
  matrix products  12.1 us (8%)
  other arithmetic  6.57 us (4%)
    unnamed x7, waiting for transfers between devices  26.1 us
    psum x1, waiting for transfers between devices, reduce_grads(): lax.psum(shards[0].astype(jnp.bfloat16), 'grp').astype(jnp.float32)  25.7 us
    reduce_scatter x1, waiting for transfers between devices, reduce_grads(): lax.psum_scatter(along_seq[0].astype(jnp.bfloat16), 'dp', scatter_dimensi...  19.4 us
    psum x1, waiting for transfers between devices, reduce_grads(): lax.psum(grads[0].astype(jnp.bfloat16), 'seq').astype(jnp.float32)  16.4 us
    unnamed x23, local copies, waits for them, and re-layouts  13.8 us
    all_gather x1, blocking collectives, teacher_attention(): key_piece = lax.all_gather(teacher_next_key, 'seq', axis=1, tiled=True)  5.65 us
    all_gather x1, blocking collectives, teacher_attention(): value_piece = lax.all_gather(teacher_next_value, 'seq', axis=1, tiled=True)  5.64 us
    all_gather x1, blocking collectives, teacher_attention(): pos_piece = lax.all_gather(positions, 'seq', axis=1, tiled=True)  5.2 us
  transfers between devices with their start and end apart: 5, of which 5 were waited for; matrix products, arithmetic and copies ran while one was open for 12% of the time, Pallas kernels for 0%

commit v1 on v0

v1 whole, which is shorter than its diff:
```python
import math

import jax
import jax.numpy as jnp
from jax import lax
from jax.experimental import pallas as pl
from jax.experimental.pallas import tpu as pltpu
from jax.sharding import PartitionSpec as P

HEAD = 128
F = 64
ADAPTER_SCALE = 2.0
MASKED = -1e30
F32 = jnp.float32
BF16 = jnp.bfloat16


def dot(a, b, ca, cb):
    return lax.dot_general(a, b, (((ca,), (cb,)), ((), ())), preferred_element_type=F32)


def student_kernel(parts, q_hbm, fw_hbm, cot_hbm, x_hbm, dw_hbm, uw_hbm, out_ref,
                   q_ref, fw_ref, cot_ref, x_ref, dw_ref, uw_ref, dq_ref, gf_ref, gd_ref, up_ref, sems):
    copies = [
        pltpu.make_async_copy(src, dst, sems.at[i])
        for i, (src, dst) in enumerate((
            (fw_hbm, fw_ref), (q_hbm, q_ref), (cot_hbm, cot_ref),
            (dw_hbm, dw_ref), (uw_hbm, uw_ref), (x_hbm, x_ref)))
    ]
    for c in copies:
        c.start()
    for c in copies[:3]:
        c.wait()
    rows = q_ref.shape[0]
    pairs = fw_ref.shape[1] // (2 * F)
    low_w = lax.broadcasted_iota(jnp.int32, (HEAD, 2 * F), 1) < F
    low = lax.broadcasted_iota(jnp.int32, (rows, 2 * F), 1) < F

    def halves(op, value, fill):
        a = op(jnp.where(low, value, fill), axis=-1, keepdims=True)
        b = op(jnp.where(low, fill, value), axis=-1, keepdims=True)
        return jnp.where(low, a, b)

    def doubled_gradient(q, w, cot):
        z = dot(q, w, 1, 0)
        e = jnp.exp(z - halves(jnp.max, z, -jnp.inf))
        prob = e / halves(jnp.sum, e, 0.0)
        g = prob * (cot - halves(jnp.sum, prob * cot, 0.0))
        return g - pltpu.roll(g, F, 1)

    for p in range(pairs):
        w_pair = fw_ref[:, p * 2 * F:(p + 1) * 2 * F].astype(F32)
        w_roll = pltpu.roll(w_pair, F, 1)
        w_first = jnp.where(low_w, w_pair, -w_roll).astype(BF16)
        w_second = jnp.where(low_w, w_roll, -w_pair).astype(BF16)
        at = 2 * p * HEAD
        q_pair = q_ref[:, at:at + 2 * HEAD]
        cot = cot_ref[:, at:at + 2 * HEAD].astype(F32)
        first = doubled_gradient(q_pair[:, :HEAD], w_first, cot[:, :HEAD])
        second = doubled_gradient(q_pair[:, HEAD:], w_second, cot[:, HEAD:])
        d_pair = jnp.where(low, first, -second).astype(BF16)
        both = dot(q_pair, d_pair, 0, 0)
        gf_ref[:, p * 2 * F:(p + 1) * 2 * F] = jnp.where(low_w, both[:HEAD], both[HEAD:])
        w_top = jnp.where(low_w, w_pair, 0.0).astype(BF16)
        w_bottom = jnp.where(low_w, 0.0, w_pair).astype(BF16)
        dq_ref[:, at:at + HEAD] = dot(d_pair, w_top, 1, 1).astype(BF16)
        dq_ref[:, at + HEAD:at + 2 * HEAD] = dot(d_pair, w_bottom, 1, 1).astype(BF16)

    for c in copies[3:]:
        c.wait()
    dq = dq_ref[...]
    x = x_ref[...]
    down = dot(x, dw_ref[...], 1, 1).astype(BF16)
    up_ref[...] = ADAPTER_SCALE * dot(down, dq, 0, 0)
    low_grad = (ADAPTER_SCALE * dot(dq, uw_ref[...], 1, 1)).astype(BF16)
    gd_ref[...] = dot(low_grad, x, 0, 0)

    width = out_ref.shape[2]
    gd_part = gd_ref.shape[1] // parts
    up_part = up_ref.shape[1] // parts
    gf_part = gf_ref.shape[0] // parts
    rank = gd_ref.shape[0]

    def padded(v):
        if v.shape[1] == width:
            return v
        return jnp.concatenate([v, jnp.zeros((v.shape[0], width - v.shape[1]), F32)], axis=1)

    for k in range(parts):
        small = jnp.concatenate([
            padded(gd_ref[:, k * gd_part:(k + 1) * gd_part]),
            padded(up_ref[:, k * up_part:(k + 1) * up_part])], axis=0)
        out_ref[k, :2 * rank, :] = small.astype(BF16)
        out_ref[k, 2 * rank:, :] = gf_ref[k * gf_part:(k + 1) * gf_part, :].astype(BF16)


def student(parts, x, q, cot, fw, dw, uw):
    rows = x.shape[0] * x.shape[1]
    x, q, cot = (v.reshape(rows, v.shape[-1]) for v in (x, q, cot))
    rank = dw.shape[0]
    width = max(fw.shape[1], x.shape[1] // parts)
    shape = (parts, 2 * rank + HEAD // parts, width)
    any_space = pl.BlockSpec(memory_space=pl.ANY)
    operands = (q, fw, cot, x, dw, uw)
    return pl.pallas_call(
        lambda *refs: student_kernel(parts, *refs),
        out_shape=jax.ShapeDtypeStruct(shape, BF16),
        in_specs=[any_space] * 6,
        out_specs=pl.BlockSpec(memory_space=pltpu.VMEM),
        scratch_shapes=[pltpu.VMEM(v.shape, BF16) for v in operands] + [
            pltpu.VMEM((rows, q.shape[1]), BF16),
            pltpu.VMEM(fw.shape, F32),
            pltpu.VMEM(dw.shape, F32),
            pltpu.VMEM(uw.shape, F32),
            pltpu.SemaphoreType.DMA((6,)),
        ],
        name="student",
    )(*operands)


def teacher_kernel(blocks, group, aliased, *refs):
    qpos_ref, kpos_ref, q_ref = refs[:3]
    k_refs = refs[3:3 + blocks]
    v_refs = refs[3 + blocks:3 + 2 * blocks]
    o_ref, bias_ref = refs[-2:]
    scale = HEAD ** -0.5 * math.log2(math.e)
    bias_ref[...] = jnp.where(kpos_ref[...] <= qpos_ref[...], 0.0, MASKED)
    keys = jnp.concatenate([k[0] for k in k_refs], axis=0)
    values = jnp.concatenate([v[0] for v in v_refs], axis=0)
    for g in range(group):
        q = q_ref[0, :, g * HEAD:(g + 1) * HEAD]
        s = dot(q, keys, 1, 1) + bias_ref[...]
        m = jnp.max(s, axis=-1, keepdims=True)
        w = jnp.exp2((s - m) * scale)
        denom = jnp.sum(w, axis=-1, keepdims=True)
        o = dot(w.astype(BF16), values, 1, 0)
        o_ref[0, :, g * HEAD:(g + 1) * HEAD] = (o * (1.0 / denom)).astype(BF16)


def teacher(q, keys, values, qpos, kpos, first, count, previous):
    blocks = len(keys)
    _, rows, key_width = keys[0].shape
    kv_heads = key_width // HEAD
    group = q.shape[2] // HEAD // kv_heads
    q_spec = pl.BlockSpec((1, q.shape[1], group * HEAD), lambda c: (0, 0, c + first))
    kv_spec = pl.BlockSpec((1, rows, HEAD), lambda c: (0, 0, c + first))
    whole = lambda v: pl.BlockSpec(v.shape, lambda c: (0, 0))
    operands = [qpos, kpos, q, *keys, *values]
    in_specs = [whole(qpos), whole(kpos), q_spec] + [kv_spec] * (2 * blocks)
    aliases = {}
    if previous is not None:
        aliases = {len(operands): 0}
        operands.append(previous)
        in_specs.append(pl.BlockSpec(memory_space=pl.ANY))
    return pl.pallas_call(
        lambda *refs: teacher_kernel(blocks, group, previous is not None, *refs),
        out_shape=jax.ShapeDtypeStruct(q.shape, BF16),
        grid=(count,),
        in_specs=in_specs,
        out_specs=q_spec,
        scratch_shapes=[pltpu.VMEM((q.shape[1], rows * blocks), F32)],
        input_output_aliases=aliases,
        name=f"teacher{first}",
    )(*operands)


def rotate(value, axis, size, shift):
    return lax.ppermute(value, axis, [(k, (k + shift) % size) for k in range(size)])


def exchange(value, axis, size, stride):
    return lax.ppermute(value, axis, [(k, k ^ stride) for k in range(size)])


def make_on_device(sizes):
    seq, dp, grp = sizes["seq"], sizes["dp"], sizes["grp"]

    def on_device(x, sq, cot, fw, dw, uw, tq, tk, tv, positions):
        pack = [(rotate(tk, "seq", seq, s), rotate(tv, "seq", seq, s), rotate(positions, "seq", seq, s))
                for s in range(1, seq)]
        keys = [tk] + [v[0] for v in pack]
        values = [tv] + [v[1] for v in pack]
        kpos = jnp.concatenate([positions] + [v[2] for v in pack], axis=1)
        qpos = positions.reshape(-1, 1)

        grads = student(dp, x, sq, cot, fw, dw, uw)
        mine = lax.axis_index("dp")
        kept = lax.dynamic_index_in_dim(grads, mine, 0, False)
        total = kept.astype(F32)
        for s in range(1, dp):
            piece = lax.dynamic_index_in_dim(grads, (mine + s) % dp, 0, False)
            total = total + rotate(piece, "dp", dp, s).astype(F32)

        kv_heads = tk.shape[2] // HEAD
        out = None
        for c in range(kv_heads):
            out = teacher(tq, keys, values, qpos, kpos, c, 1, out)

        for axis, size in (("seq", seq), ("grp", grp)):
            stride = 1
            while stride < size:
                total = total + exchange(total.astype(BF16), axis, size, stride).astype(F32)
                stride *= 2
        rank = dw.shape[0]
        grad_down = total[:rank, :x.shape[2] // dp]
        up = total[rank:2 * rank, :sq.shape[2] // dp]
        grad_feature = total[2 * rank:, :fw.shape[1]]
        return out, grad_feature, grad_down, up

    return on_device


def solution(mesh):
    tokens = P(("grp", "dp"), "seq", None)
    return jax.shard_map(
        make_on_device(dict(mesh.shape)),
        mesh=mesh,
        in_specs=(tokens, tokens, tokens, P(), P(), P(), tokens, tokens, tokens, P(("grp", "dp"), "seq")),
        out_specs=(tokens, P("dp", None), P(None, "dp"), P(None, "dp")),
        check_vma=False,
    )
```

time: 153 us -> 44.8 us (0.29)
  waiting for transfers between devices: 87.6 us -> 10.2 us
  blocking collectives: 16.5 us -> 0 us
  Pallas kernels: 0 us -> 16.2 us
  between operations: 14 us -> 0.74 us
  matrix products: 12.1 us -> 0 us
  starting transfers between devices: 0.2 us -> 12 us
  local copies, waits for them, and re-layouts: 16 us -> 4.36 us
  other arithmetic: 6.57 us -> 1.04 us
    psum x2 -> x0, waiting for transfers between devices: 42.1 us -> none  [the longest x1 25.7 us: reduce_grads(): lax.psum(shards[0].astype(jnp.bfloat16), 'grp').astype(jnp.float32)]
    unnamed x7 -> x0, waiting for transfers between devices: 26.1 us -> none
    reduce_scatter x1 -> x0, waiting for transfers between devices: 19.4 us -> none  [reduce_grads(): lax.psum_scatter(along_seq[0].astype(jnp.bfloat16), 'dp', scatter_dimensi...]
    all_gather x3 -> x0, blocking collectives: 16.5 us -> none  [the longest x1 5.65 us: teacher_attention(): key_piece = lax.all_gather(teacher_next_key, 'seq', axis=1, tiled=True)]
    pallas_call x0 -> x3, Pallas kernels: none -> 16.2 us  [the longest x2 8.57 us: teacher(): pl.pallas_call(lambda *refs: teacher_kernel(blocks, group, previous is no...]
    unnamed x23 -> x13, local copies, waits for them, and re-layouts: 13.8 us -> 0.68 us
    ppermute x0 -> x9, starting transfers between devices: none -> 12 us  [the longest x6 8.77 us: rotate(): lax.ppermute(value, axis, [(k, (k + shift) % size) for k in range(size)])]
    dot_general x6 -> x0, matrix products: 10.7 us -> none  [the longest x1 5.15 us: one_block(): jnp.einsum('cgqk,kcd->qcgd', weights.astype(jnp.bfloat16), rows_of_values...]
  transfers between devices with their start and end apart: 5 -> 9, of which waited for: 5 -> 5; matrix products, arithmetic and copies ran while one was open for 12% -> 2% of each run, Pallas kernels for 0% -> 19%
where the time goes in v1:
time: 44.8 us; the launch traced here: 44.6 us
  Pallas kernels  16.2 us (36%)
  starting transfers between devices  12 us (27%)
  waiting for transfers between devices  10.2 us (23%)
  local copies, waits for them, and re-layouts  4.36 us (10%)
  other arithmetic  1.04 us (2%)
  between operations  0.74 us (2%)
    ppermute x6, waiting for transfers between devices, rotate(): lax.ppermute(value, axis, [(k, (k + shift) % size) for k in range(size)])  8.98 us
    ppermute x6, starting transfers between devices, rotate(): lax.ppermute(value, axis, [(k, (k + shift) % size) for k in range(size)])  8.77 us
    pallas_call x2, Pallas kernels, teacher(): pl.pallas_call(lambda *refs: teacher_kernel(blocks, group, previous is no...  8.57 us
    pallas_call x1, Pallas kernels, student(): pl.pallas_call(lambda *refs: student_kernel(parts, *refs), out_shape=jax....  7.61 us
    ppermute x3, starting transfers between devices, exchange(): return lax.ppermute(value, axis, [(k, k ^ stride) for k in range(size)])  3.22 us
    ppermute x3, waiting for transfers between devices, exchange(): return lax.ppermute(value, axis, [(k, k ^ stride) for k in range(size)])  1.26 us
    squeeze x1, local copies, waits for them, and re-layouts, on_device(): piece = lax.dynamic_index_in_dim(grads, (mine + s) % dp, 0, False)  1 us
    convert_element_type x3, other arithmetic, on_device(): total = total + exchange(total.astype(BF16), axis, size, stride).astype(F32)  1 us
  transfers between devices with their start and end apart: 9, of which 5 were waited for; matrix products, arithmetic and copies ran while one was open for 2% of the time, Pallas kernels for 19%

profile of v1, /device:TPU:0, one launch (start us, length us, event | category | flops | bytes accessed | tf_op | source)
XLA Modules:
  0.0 44.6 jit_solution(4571377662570785124)
XLA Ops:
  0.7 7.6 %student.1 = bf16[4,48,896]{2,1,0:T(8,128)(2,1)} custom-call(bf16[128,1792]{1,0:T(8,128)(2,1)} %bitcast.15, bf16[128,896]{1,0:T(8,128)(2,1)} %refs_1_.1, bf16[128,1792]{1,0:T(8,128)(2,1)} %bitcast.16, bf16[128,3584]{1,0:T(8,128)(2,1)} %bitcast.14, bf16[8,3584]{1,0:T(8,128)(2,1)} %refs_4_.1, bf16[8,1792]{1,0:T(8,128)(2,1)} %refs_5_.5), custom_call_target="tpu_custom_call" | custom-call | tf_op jit(solution)/shard_map/student/pallas_call | solution.py:105
  8.3 1.0 %dynamic-slice_bitcast_fusion.2 = (bf16[48,896]{1,0:T(8,128)(2,1)S(1)}, bf16[48,896]{1,0:T(8,128)(2,1)S(1)}, bf16[48,896]{1,0:T(8,128)(2,1)S(1)}) fusion(bf16[4,48,896]{2,1,0:T(8,128)(2,1)} %student.1, s32[]{:T(128)S(6)} %select_n.30, s32[]{:T(128)S(6)} %select_n.34, s32[]{:T(128)S(6)} %select_n.32), kind=kLoop, calls=%fused_computation.9 | loop fusion | bytes 516108 | tf_op jit(solution)/shard_map/jit(dynamic_index_in_dim)/squeeze | solution.py:191
  9.3 5.1 %collective-permute-start.5 = (bf16[48,896]{1,0:T(8,128)(2,1)S(1)}, bf16[48,896]{1,0:T(8,128)(2,1)S(1)}, u32[]{:S(2)}, u32[]{:S(2)}) collective-permute-start(bf16[48,896]{1,0:T(8,128)(2,1)S(1)} %get-tuple-element.7), channel_id=1, source_target_pairs={{0,6},{2,0},{4,2},{6,4},{1,7},{3,1},{5,3},{7,5},{8,14},{10,8},{12,... | collective-permute-start | bytes 258056 | tf_op jit(solution)/shard_map/ppermute | solution.py:168
  14.4 0.0 collective-permute-start.4
  14.4 1.0 %collective-permute-start.3 = (bf16[48,896]{1,0:T(8,128)(2,1)S(1)}, bf16[48,896]{1,0:T(8,128)(2,1)S(1)}, u32[]{:S(2)}, u32[]{:S(2)}) collective-permute-start(bf16[48,896]{1,0:T(8,128)(2,1)S(1)} %get-tuple-element.6), channel_id=1, source_target_pairs={{0,2},{2,4},{4,6},{6,0},{1,3},{3,5},{5,7},{7,1},{8,10},{10,12},{12... | collective-permute-start | bytes 258056 | tf_op jit(solution)/shard_map/ppermute | solution.py:168
  15.4 0.0 copy-start
  15.4 0.0 copy-start.1
  15.4 1.9 %collective-permute-done.5 = bf16[48,896]{1,0:T(8,128)(2,1)S(1)} collective-permute-done((bf16[48,896]{1,0:T(8,128)(2,1)S(1)}, bf16[48,896]{1,0:T(8,128)(2,1)S(1)}, u32[]{:S(2)}, u32[]{:S(2)}) %collective-permute-start.5) | collective-permute-done | bytes 86048 | tf_op jit(solution)/shard_map/ppermute | solution.py:168
  17.3 4.9 %collective-permute-done.4 = bf16[48,896]{1,0:T(8,128)(2,1)S(1)} collective-permute-done((bf16[48,896]{1,0:T(8,128)(2,1)S(1)}, bf16[48,896]{1,0:T(8,128)(2,1)S(1)}, u32[]{:S(2)}, u32[]{:S(2)}) %collective-permute-start.4) | collective-permute-done | bytes 86048 | tf_op jit(solution)/shard_map/ppermute | solution.py:168
  22.3 0.0 collective-permute-done.3
  22.3 0.9 %fusion.4 = (bf16[48,896]{1,0:T(8,128)(2,1)S(1)}, f32[48,896]{1,0:T(8,128)S(1)}) fusion(bf16[48,896]{1,0:T(8,128)(2,1)S(1)} %collective-permute-done.5, bf16[48,896]{1,0:T(8,128)(2,1)S(1)} %collective-permute-done.4, bf16[48,896]{1,0:T(8,128)(2,1)S(1)} %collective-permute-done.3, bf16[4,48,896]{2,1,0:T(8,128)(2,1)} %student.1, s32[]{:T(128)S(6)} %select_n.28), kind=kLoop, calls=%fused_computation.13 | loop fusion | flops 344064 | bytes 602116 | tf_op jit(solution)/shard_map/convert_element_type | solution.py:202
  23.2 0.0 copy-start.5
  23.2 1.6 %collective-permute-start.6 = (bf16[48,896]{1,0:T(8,128)(2,1)S(1)}, bf16[48,896]{1,0:T(8,128)(2,1)S(1)}, u32[]{:S(2)}, u32[]{:S(2)}) collective-permute-start(bf16[48,896]{1,0:T(8,128)(2,1)S(1)} %get-tuple-element.4), channel_id=1, source_target_pairs={{0,1},{1,0},{2,3},{3,2},{4,5},{5,4},{6,7},{7,6},{8,9},{9,8},{10,11... | collective-permute-start | bytes 258056 | tf_op jit(solution)/shard_map/ppermute | solution.py:172
  24.8 0.0 copy-done.5
  24.8 0.6 %collective-permute-start = (s32[1,256]{1,0:T(1,128)S(1)}, s32[1,256]{1,0:T(1,128)S(1)}, u32[]{:S(2)}, u32[]{:S(2)}) collective-permute-start(s32[1,256]{1,0:T(1,128)S(1)} %copy-done.5), channel_id=1, source_target_pairs={{0,1},{1,0},{2,3},{3,2},{4,5},{5,4},{6,7},{7,6},{8,9},{9,8},{10,11... | collective-permute-start | bytes 3080 | tf_op jit(solution)/shard_map/ppermute | solution.py:168
  25.4 0.0 copy-done
  25.4 1.4 %collective-permute-start.1 = (bf16[1,256,256]{2,1,0:T(8,128)(2,1)S(1)}, bf16[1,256,256]{2,1,0:T(8,128)(2,1)S(1)}, u32[]{:S(2)}, u32[]{:S(2)}) collective-permute-start(bf16[1,256,256]{2,1,0:T(8,128)(2,1)S(1)} %copy-done), channel_id=1, source_target_pairs={{0,1},{1,0},{2,3},{3,2},{4,5},{5,4},{6,7},{7,6},{8,9},{9,8},{10,11... | collective-permute-start | bytes 393224 | tf_op jit(solution)/shard_map/ppermute | solution.py:168
  26.8 0.0 copy-done.1
  26.8 0.6 %collective-permute-start.2 = (bf16[1,256,256]{2,1,0:T(8,128)(2,1)S(1)}, bf16[1,256,256]{2,1,0:T(8,128)(2,1)S(1)}, u32[]{:S(2)}, u32[]{:S(2)}) collective-permute-start(bf16[1,256,256]{2,1,0:T(8,128)(2,1)S(1)} %copy-done.1), channel_id=1, source_target_pairs={{0,1},{1,0},{2,3},{3,2},{4,5},{5,4},{6,7},{7,6},{8,9},{9,8},{10,11... | collective-permute-start | bytes 393224 | tf_op jit(solution)/shard_map/ppermute | solution.py:168
  27.4 0.8 %copy.16.refs_0_ = s32[256,1]{1,0:T(8,128)} copy(s32[256,1]{0,1:T(1,128)S(1)} %bitcast.17) | data formatting | bytes 2048 | tf_op jit(solution)/shard_map/reshape | solution.py:184
  28.2 0.0 collective-permute-done.6
  28.3 0.1 collective-permute-start.7
  28.4 1.3 %collective-permute-done.7 = bf16[48,896]{1,0:T(8,128)(2,1)S(1)} collective-permute-done((bf16[48,896]{1,0:T(8,128)(2,1)S(1)}, bf16[48,896]{1,0:T(8,128)(2,1)S(1)}, u32[]{:S(2)}, u32[]{:S(2)}) %collective-permute-start.7) | collective-permute-done | bytes 86048 | tf_op jit(solution)/shard_map/ppermute | solution.py:172
  29.7 1.6 %collective-permute-start.8 = (bf16[48,896]{1,0:T(8,128)(2,1)S(1)}, bf16[48,896]{1,0:T(8,128)(2,1)S(1)}, u32[]{:S(2)}, u32[]{:S(2)}) collective-permute-start(bf16[48,896]{1,0:T(8,128)(2,1)S(1)} %fusion.3), channel_id=1, source_target_pairs={{0,16},{8,24},{16,0},{24,8},{1,17},{9,25},{17,1},{25,9},{2,18},{10... | collective-permute-start | bytes 258056 | tf_op jit(solution)/shard_map/ppermute | solution.py:172
  31.2 0.0 collective-permute-done
  31.2 0.0 copy-start.4
  31.2 0.5 %collective-permute-done.1.refs_4_ = bf16[1,256,256]{2,1,0:T(8,128)(2,1)S(1)} collective-permute-done((bf16[1,256,256]{2,1,0:T(8,128)(2,1)S(1)}, bf16[1,256,256]{2,1,0:T(8,128)(2,1)S(1)}, u32[]{:S(2)}, u32[]{:S(2)}) %collective-permute-start.1) | collective-permute-done | bytes 131104 | tf_op jit(solution)/shard_map/ppermute | solution.py:168
  31.8 0.0 copy-start.2
  31.8 1.6 %collective-permute-done.2.refs_6_ = bf16[1,256,256]{2,1,0:T(8,128)(2,1)S(1)} collective-permute-done((bf16[1,256,256]{2,1,0:T(8,128)(2,1)S(1)}, bf16[1,256,256]{2,1,0:T(8,128)(2,1)S(1)}, u32[]{:S(2)}, u32[]{:S(2)}) %collective-permute-start.2) | collective-permute-done | bytes 131104 | tf_op jit(solution)/shard_map/ppermute | solution.py:168
  33.4 0.0 copy-done.4
  33.4 0.0 copy-done.2
  33.4 0.0 copy-start.3
  33.4 0.7 %copy-done.3 = bf16[1,256,256]{2,1,0:T(8,128)(2,1)} copy-done((bf16[1,256,256]{2,1,0:T(8,128)(2,1)}, bf16[1,256,256]{2,1,0:T(8,128)(2,1)S(1)}, u32[]{:S(2)}) %copy-start.3) | copy-done | bytes 131096
  34.1 4.3 %teacher0.1.refs_7_ = bf16[1,256,1792]{2,1,0:T(8,128)(2,1)} custom-call(s32[256,1]{1,0:T(8,128)} %copy.16.refs_0_, s32[1,512]{1,0:T(1,128)} %copy-done.4, bf16[1,256,1792]{2,1,0:T(8,128)(2,1)} %refs_2_.3, bf16[1,256,256]{2,1,0:T(8,128)(2,1)} %refs_3_.3, bf16[1,256,256]{2,1,0:T(8,128)(2,1)} %copy-done.2, bf16[1,256,256]{2,1,0:T(8,128)(2,1)} %refs_5_.4, ...), custom_call_target="tpu_custom_call" | custom-call | tf_op jit(solution)/shard_map/teacher0/pallas_call | solution.py:155
  38.3 4.3 %teacher1.1 = bf16[1,256,1792]{2,1,0:T(8,128)(2,1)} custom-call(s32[256,1]{1,0:T(8,128)} %copy.16.refs_0_, s32[1,512]{1,0:T(1,128)} %copy-done.4, bf16[1,256,1792]{2,1,0:T(8,128)(2,1)} %refs_2_.3, bf16[1,256,256]{2,1,0:T(8,128)(2,1)} %refs_3_.3, bf16[1,256,256]{2,1,0:T(8,128)(2,1)} %copy-done.2, ...), custom_call_target="tpu_custom_call", output_to_operand_aliasing={{}: (7, {})} | custom-call | tf_op jit(solution)/shard_map/teacher1/pallas_call | solution.py:155
  42.6 0.0 collective-permute-done.8
  42.7 0.7 %slice.12 = f32[32,896]{1,0:T(8,128)} slice(f32[48,896]{1,0:T(8,128)S(1)} %convert_add_fusion.1), slice={[16:48], [0:896]} | slice | bytes 229376 | tf_op jit(solution)/shard_map/slice | solution.py:207
  43.3 0.6 %slice.13 = f32[8,896]{1,0:T(8,128)} slice(f32[48,896]{1,0:T(8,128)S(1)} %convert_add_fusion.1), slice={[0:8], [0:896]} | slice | bytes 57344 | tf_op jit(solution)/shard_map/slice | solution.py:205
  43.9 0.6 %slice.14 = f32[8,448]{1,0:T(8,128)} slice(f32[48,896]{1,0:T(8,128)S(1)} %convert_add_fusion.1), slice={[8:16], [0:448]} | slice | bytes 28672 | tf_op jit(solution)/shard_map/slice | solution.py:206
  (5 shorter events, 0.1 us)
Async XLA Ops:
  9.3 8.0 %collective-permute-start.5 = (bf16[48,896]{1,0:T(8,128)(2,1)S(1)}, bf16[48,896]{1,0:T(8,128)(2,1)S(1)}, u32[]{:S(2)}, u32[]{:S(2)}) collective-permute-start(bf16[48,896]{1,0:T(8,128)(2,1)S(1)} %get-tuple-element.7), channel_id=1, source_target_pairs={{0,6},{2,0},{4,2},{6,4},{1,7},{3,1},{5,3},{7,5},{8,14},{10,8},{12,... | collective-permute-start | bytes 258056 | tf_op jit(solution)/shard_map/ppermute | solution.py:168
  14.4 7.8 %collective-permute-start.4 = (bf16[48,896]{1,0:T(8,128)(2,1)S(1)}, bf16[48,896]{1,0:T(8,128)(2,1)S(1)}, u32[]{:S(2)}, u32[]{:S(2)}) collective-permute-start(bf16[48,896]{1,0:T(8,128)(2,1)S(1)} %get-tuple-element.8), channel_id=1, source_target_pairs={{0,4},{2,6},{4,0},{6,2},{1,5},{3,7},{5,1},{7,3},{8,12},{10,14},{12... | collective-permute-start | bytes 258056 | tf_op jit(solution)/shard_map/ppermute | solution.py:168
  14.4 7.8 %collective-permute-start.3 = (bf16[48,896]{1,0:T(8,128)(2,1)S(1)}, bf16[48,896]{1,0:T(8,128)(2,1)S(1)}, u32[]{:S(2)}, u32[]{:S(2)}) collective-permute-start(bf16[48,896]{1,0:T(8,128)(2,1)S(1)} %get-tuple-element.6), channel_id=1, source_target_pairs={{0,2},{2,4},{4,6},{6,0},{1,3},{3,5},{5,7},{7,1},{8,10},{10,12},{12... | collective-permute-start | bytes 258056 | tf_op jit(solution)/shard_map/ppermute | solution.py:168
  15.4 10.0 %copy-start = (bf16[1,256,256]{2,1,0:T(8,128)(2,1)S(1)}, bf16[1,256,256]{2,1,0:T(8,128)(2,1)}, u32[]{:S(2)}) copy-start(bf16[1,256,256]{2,1,0:T(8,128)(2,1)} %refs_3_.3) | copy-start | bytes 393220
  15.4 11.4 %copy-start.1 = (bf16[1,256,256]{2,1,0:T(8,128)(2,1)S(1)}, bf16[1,256,256]{2,1,0:T(8,128)(2,1)}, u32[]{:S(2)}) copy-start(bf16[1,256,256]{2,1,0:T(8,128)(2,1)} %refs_5_.4) | copy-start | bytes 393220
  23.2 1.6 %copy-start.5 = (s32[1,256]{1,0:T(1,128)S(1)}, s32[1,256]{1,0:T(1,128)}, u32[]{:S(2)}) copy-start(s32[1,256]{1,0:T(1,128)} %param.19) | copy-start | bytes 3076
  23.2 5.0 %collective-permute-start.6 = (bf16[48,896]{1,0:T(8,128)(2,1)S(1)}, bf16[48,896]{1,0:T(8,128)(2,1)S(1)}, u32[]{:S(2)}, u32[]{:S(2)}) collective-permute-start(bf16[48,896]{1,0:T(8,128)(2,1)S(1)} %get-tuple-element.4), channel_id=1, source_target_pairs={{0,1},{1,0},{2,3},{3,2},{4,5},{5,4},{6,7},{7,6},{8,9},{9,8},{10,11... | collective-permute-start | bytes 258056 | tf_op jit(solution)/shard_map/ppermute | solution.py:172
  24.8 6.4 %collective-permute-start = (s32[1,256]{1,0:T(1,128)S(1)}, s32[1,256]{1,0:T(1,128)S(1)}, u32[]{:S(2)}, u32[]{:S(2)}) collective-permute-start(s32[1,256]{1,0:T(1,128)S(1)} %copy-done.5), channel_id=1, source_target_pairs={{0,1},{1,0},{2,3},{3,2},{4,5},{5,4},{6,7},{7,6},{8,9},{9,8},{10,11... | collective-permute-start | bytes 3080 | tf_op jit(solution)/shard_map/ppermute | solution.py:168
  25.4 6.4 %collective-permute-start.1 = (bf16[1,256,256]{2,1,0:T(8,128)(2,1)S(1)}, bf16[1,256,256]{2,1,0:T(8,128)(2,1)S(1)}, u32[]{:S(2)}, u32[]{:S(2)}) collective-permute-start(bf16[1,256,256]{2,1,0:T(8,128)(2,1)S(1)} %copy-done), channel_id=1, source_target_pairs={{0,1},{1,0},{2,3},{3,2},{4,5},{5,4},{6,7},{7,6},{8,9},{9,8},{10,11... | collective-permute-start | bytes 393224 | tf_op jit(solution)/shard_map/ppermute | solution.py:168
  26.8 6.6 %collective-permute-start.2 = (bf16[1,256,256]{2,1,0:T(8,128)(2,1)S(1)}, bf16[1,256,256]{2,1,0:T(8,128)(2,1)S(1)}, u32[]{:S(2)}, u32[]{:S(2)}) collective-permute-start(bf16[1,256,256]{2,1,0:T(8,128)(2,1)S(1)} %copy-done.1), channel_id=1, source_target_pairs={{0,1},{1,0},{2,3},{3,2},{4,5},{5,4},{6,7},{7,6},{8,9},{9,8},{10,11... | collective-permute-start | bytes 393224 | tf_op jit(solution)/shard_map/ppermute | solution.py:168
  28.3 1.3 %collective-permute-start.7 = (bf16[48,896]{1,0:T(8,128)(2,1)S(1)}, bf16[48,896]{1,0:T(8,128)(2,1)S(1)}, u32[]{:S(2)}, u32[]{:S(2)}) collective-permute-start(bf16[48,896]{1,0:T(8,128)(2,1)S(1)} %fusion.2), channel_id=1, source_target_pairs={{0,8},{8,0},{16,24},{24,16},{1,9},{9,1},{17,25},{25,17},{2,10},{10... | collective-permute-start | bytes 258056 | tf_op jit(solution)/shard_map/ppermute | solution.py:172
  29.7 13.0 %collective-permute-start.8 = (bf16[48,896]{1,0:T(8,128)(2,1)S(1)}, bf16[48,896]{1,0:T(8,128)(2,1)S(1)}, u32[]{:S(2)}, u32[]{:S(2)}) collective-permute-start(bf16[48,896]{1,0:T(8,128)(2,1)S(1)} %fusion.3), channel_id=1, source_target_pairs={{0,16},{8,24},{16,0},{24,8},{1,17},{9,25},{17,1},{25,9},{2,18},{10... | collective-permute-start | bytes 258056 | tf_op jit(solution)/shard_map/ppermute | solution.py:172
  31.2 2.2 %copy-start.4 = (s32[1,512]{1,0:T(1,128)}, s32[1,512]{1,0:T(1,128)S(1)}, u32[]{:S(2)}) copy-start(s32[1,512]{1,0:T(1,128)S(1)} %constant_dynamic-update-slice_fusion.refs_1_) | copy-start | bytes 6148
  31.8 1.6 %copy-start.2 = (bf16[1,256,256]{2,1,0:T(8,128)(2,1)}, bf16[1,256,256]{2,1,0:T(8,128)(2,1)S(1)}, u32[]{:S(2)}) copy-start(bf16[1,256,256]{2,1,0:T(8,128)(2,1)S(1)} %collective-permute-done.1.refs_4_) | copy-start | bytes 393220
  33.4 0.7 %copy-start.3 = (bf16[1,256,256]{2,1,0:T(8,128)(2,1)}, bf16[1,256,256]{2,1,0:T(8,128)(2,1)S(1)}, u32[]{:S(2)}) copy-start(bf16[1,256,256]{2,1,0:T(8,128)(2,1)S(1)} %collective-permute-done.2.refs_6_) | copy-start | bytes 393220

commit v2 on v1

--- a/solution.py
+++ b/solution.py
@@ -19,8 +19,8 @@
     return lax.dot_general(a, b, (((ca,), (cb,)), ((), ())), preferred_element_type=F32)
 
 
-def student_kernel(parts, q_hbm, fw_hbm, cot_hbm, x_hbm, dw_hbm, uw_hbm, out_ref,
-                   q_ref, fw_ref, cot_ref, x_ref, dw_ref, uw_ref, dq_ref, gf_ref, gd_ref, up_ref, sems):
+def student_kernel(parts, q_hbm, fw_hbm, cot_hbm, x_hbm, dw_hbm, uw_hbm, pack_ref,
+                   q_ref, fw_ref, cot_ref, x_ref, dw_ref, uw_ref, dq_ref, gd_ref, up_ref, sems):
     copies = [
         pltpu.make_async_copy(src, dst, sems.at[i])
         for i, (src, dst) in enumerate((
@@ -31,40 +31,41 @@
         c.start()
     for c in copies[:3]:
         c.wait()
-    rows = q_ref.shape[0]
     pairs = fw_ref.shape[1] // (2 * F)
+    rank = gd_ref.shape[0]
+    gf_part = HEAD // parts
     low_w = lax.broadcasted_iota(jnp.int32, (HEAD, 2 * F), 1) < F
-    low = lax.broadcasted_iota(jnp.int32, (rows, 2 * F), 1) < F
-
-    def halves(op, value, fill):
-        a = op(jnp.where(low, value, fill), axis=-1, keepdims=True)
-        b = op(jnp.where(low, fill, value), axis=-1, keepdims=True)
-        return jnp.where(low, a, b)
-
-    def doubled_gradient(q, w, cot):
-        z = dot(q, w, 1, 0)
-        e = jnp.exp(z - halves(jnp.max, z, -jnp.inf))
-        prob = e / halves(jnp.sum, e, 0.0)
-        g = prob * (cot - halves(jnp.sum, prob * cot, 0.0))
-        return g - pltpu.roll(g, F, 1)
+    eye = identity(2 * HEAD)
+
+    def side(e, cot):
+        inverse = 1.0 / jnp.sum(e, axis=0, keepdims=True)
+        mean = jnp.sum(e * cot, axis=0, keepdims=True) * inverse
+        return e * inverse * (cot - mean)
 
     for p in range(pairs):
+        at = 2 * p * HEAD
         w_pair = fw_ref[:, p * 2 * F:(p + 1) * 2 * F].astype(F32)
-        w_roll = pltpu.roll(w_pair, F, 1)
-        w_first = jnp.where(low_w, w_pair, -w_roll).astype(BF16)
-        w_second = jnp.where(low_w, w_roll, -w_pair).astype(BF16)
-        at = 2 * p * HEAD
+        w_both = jnp.concatenate(
+            [jnp.where(low_w, w_pair, 0.0), jnp.where(low_w, 0.0, w_pair)], axis=0).astype(BF16)
         q_pair = q_ref[:, at:at + 2 * HEAD]
-        cot = cot_ref[:, at:at + 2 * HEAD].astype(F32)
-        first = doubled_gradient(q_pair[:, :HEAD], w_first, cot[:, :HEAD])
-        second = doubled_gradient(q_pair[:, HEAD:], w_second, cot[:, HEAD:])
-        d_pair = jnp.where(low, first, -second).astype(BF16)
-        both = dot(q_pair, d_pair, 0, 0)
-        gf_ref[:, p * 2 * F:(p + 1) * 2 * F] = jnp.where(low_w, both[:HEAD], both[HEAD:])
-        w_top = jnp.where(low_w, w_pair, 0.0).astype(BF16)
-        w_bottom = jnp.where(low_w, 0.0, w_pair).astype(BF16)
-        dq_ref[:, at:at + HEAD] = dot(d_pair, w_top, 1, 1).astype(BF16)
-        dq_ref[:, at + HEAD:at + 2 * HEAD] = dot(d_pair, w_bottom, 1, 1).astype(BF16)
+        logit = dot(w_both, q_pair, 0, 1)
+        cot = dot(eye, cot_ref[:, at:at + 2 * HEAD], 1, 1)
+        grads = []
+        for h in range(2):
+            z = logit[h * F:(h + 1) * F]
+            cot_plus = cot[2 * h * F:(2 * h + 1) * F]
+            cot_minus = cot[(2 * h + 1) * F:(2 * h + 2) * F]
+            plus = jnp.exp(z - jnp.max(z, axis=0, keepdims=True))
+            minus = jnp.exp(jnp.min(z, axis=0, keepdims=True) - z)
+            grads.append(side(plus, cot_plus) - side(minus, cot_minus))
+        d_pair = jnp.concatenate(grads, axis=0).astype(BF16)
+        dq_ref[:, at:at + 2 * HEAD] = dot(d_pair, w_both, 0, 1).astype(BF16)
+        both = dot(d_pair, q_pair, 1, 0)
+        map_grad = jnp.concatenate([both[:F, :HEAD], both[F:, HEAD:]], axis=0).astype(BF16)
+        map_grad = dot(eye[:HEAD, :HEAD], map_grad, 1, 1)
+        for k in range(parts):
+            pack_ref[k, 2 * rank:, p * 2 * F:(p + 1) * 2 * F] = (
+                map_grad[k * gf_part:(k + 1) * gf_part].astype(BF16))
 
     for c in copies[3:]:
         c.wait()
@@ -75,11 +76,9 @@
     low_grad = (ADAPTER_SCALE * dot(dq, uw_ref[...], 1, 1)).astype(BF16)
     gd_ref[...] = dot(low_grad, x, 0, 0)
 
-    width = out_ref.shape[2]
+    width = pack_ref.shape[2]
     gd_part = gd_ref.shape[1] // parts
     up_part = up_ref.shape[1] // parts
-    gf_part = gf_ref.shape[0] // parts
-    rank = gd_ref.shape[0]
 
     def padded(v):
         if v.shape[1] == width:
@@ -90,8 +89,12 @@
         small = jnp.concatenate([
             padded(gd_ref[:, k * gd_part:(k + 1) * gd_part]),
             padded(up_ref[:, k * up_part:(k + 1) * up_part])], axis=0)
-        out_ref[k, :2 * rank, :] = small.astype(BF16)
-        out_ref[k, 2 * rank:, :] = gf_ref[k * gf_part:(k + 1) * gf_part, :].astype(BF16)
+        pack_ref[k, :2 * rank, :] = small.astype(BF16)
+
+
+def identity(n):
+    return (lax.broadcasted_iota(jnp.int32, (n, n), 0)
+            == lax.broadcasted_iota(jnp.int32, (n, n), 1)).astype(F32).astype(BF16)
 
 
 def student(parts, x, q, cot, fw, dw, uw):
@@ -109,7 +112,6 @@
         out_specs=pl.BlockSpec(memory_space=pltpu.VMEM),
         scratch_shapes=[pltpu.VMEM(v.shape, BF16) for v in operands] + [
             pltpu.VMEM((rows, q.shape[1]), BF16),
-            pltpu.VMEM(fw.shape, F32),
             pltpu.VMEM(dw.shape, F32),
             pltpu.VMEM(uw.shape, F32),
             pltpu.SemaphoreType.DMA((6,)),
@@ -118,7 +120,7 @@
     )(*operands)
 
 
-def teacher_kernel(blocks, group, aliased, *refs):
+def teacher_kernel(blocks, group, *refs):
     qpos_ref, kpos_ref, q_ref = refs[:3]
     k_refs = refs[3:3 + blocks]
     v_refs = refs[3 + blocks:3 + 2 * blocks]
@@ -153,14 +155,13 @@
         operands.append(previous)
         in_specs.append(pl.BlockSpec(memory_space=pl.ANY))
     return pl.pallas_call(
-        lambda *refs: teacher_kernel(blocks, group, previous is not None, *refs),
+        lambda *refs: teacher_kernel(blocks, group, *refs),
         out_shape=jax.ShapeDtypeStruct(q.shape, BF16),
         grid=(count,),
         in_specs=in_specs,
         out_specs=q_spec,
         scratch_shapes=[pltpu.VMEM((q.shape[1], rows * blocks), F32)],
         input_output_aliases=aliases,
-        name=f"teacher{first}",
     )(*operands)
 
 
@@ -175,9 +176,13 @@
 def make_on_device(sizes):
     seq, dp, grp = sizes["seq"], sizes["dp"], sizes["grp"]
 
-    def on_device(x, sq, cot, fw, dw, uw, tq, tk, tv, positions):
-        pack = [(rotate(tk, "seq", seq, s), rotate(tv, "seq", seq, s), rotate(positions, "seq", seq, s))
-                for s in range(1, seq)]
+    def compute(x, sq, cot, fw, dw, uw, tq, tk, tv, positions):
+        pack = []
+        for s in range(1, seq):
+            moved = []
+            for v in (tk, tv, positions):
+                moved.append(rotate(v, "seq", seq, s))
+            pack.append(moved)
         keys = [tk] + [v[0] for v in pack]
         values = [tv] + [v[1] for v in pack]
         kpos = jnp.concatenate([positions] + [v[2] for v in pack], axis=1)
@@ -185,11 +190,11 @@
 
         grads = student(dp, x, sq, cot, fw, dw, uw)
         mine = lax.axis_index("dp")
-        kept = lax.dynamic_index_in_dim(grads, mine, 0, False)
-        total = kept.astype(F32)
+        total = lax.dynamic_index_in_dim(grads, mine, 0, False).astype(F32)
         for s in range(1, dp):
             piece = lax.dynamic_index_in_dim(grads, (mine + s) % dp, 0, False)
-            total = total + rotate(piece, "dp", dp, s).astype(F32)
+            piece = rotate(piece, "dp", dp, s)
+            total = total + piece.astype(F32)
 
         kv_heads = tk.shape[2] // HEAD
         out = None
@@ -199,7 +204,8 @@
         for axis, size in (("seq", seq), ("grp", grp)):
             stride = 1
             while stride < size:
-                total = total + exchange(total.astype(BF16), axis, size, stride).astype(F32)
+                moved = exchange(total.astype(BF16), axis, size, stride)
+                total = total + moved.astype(F32)
                 stride *= 2
         rank = dw.shape[0]
         grad_down = total[:rank, :x.shape[2] // dp]
@@ -207,13 +213,14 @@
         grad_feature = total[2 * rank:, :fw.shape[1]]
         return out, grad_feature, grad_down, up
 
-    return on_device
+    return compute
 
 
 def solution(mesh):
     tokens = P(("grp", "dp"), "seq", None)
+    sizes = dict(mesh.shape)
     return jax.shard_map(
-        make_on_device(dict(mesh.shape)),
+        make_on_device(sizes),
         mesh=mesh,
         in_specs=(tokens, tokens, tokens, P(), P(), P(), tokens, tokens, tokens, P(("grp", "dp"), "seq")),
         out_specs=(tokens, P("dp", None), P(None, "dp"), P(None, "dp")),

time: 44.8 us -> 44.1 us (0.984)
  Pallas kernels: 16.2 us -> 15.4 us
    pallas_call x1, Pallas kernels: 7.61 us -> 6.84 us  [student(): pl.pallas_call(lambda *refs: student_kernel(parts, *refs), out_shape=jax....]
  transfers between devices with their start and end apart: 9 -> 9, of which waited for: 5 -> 5; matrix products, arithmetic and copies ran while one was open for 2% -> 2% of each run, Pallas kernels for 19% -> 20%
where the time goes in v2:
time: 44.1 us; the launch traced here: 43.8 us
  Pallas kernels  15.4 us (35%)
  starting transfers between devices  12 us (27%)
  waiting for transfers between devices  10.2 us (23%)
  local copies, waits for them, and re-layouts  4.36 us (10%)
  other arithmetic  1.04 us (2%)
  between operations  0.74 us (2%)
    ppermute x6, waiting for transfers between devices, rotate(): lax.ppermute(value, axis, [(k, (k + shift) % size) for k in range(size)])  8.98 us
    ppermute x6, starting transfers between devices, rotate(): lax.ppermute(value, axis, [(k, (k + shift) % size) for k in range(size)])  8.77 us
    pallas_call x2, Pallas kernels, teacher(): pl.pallas_call(lambda *refs: teacher_kernel(blocks, group, *refs), out_sh...  8.57 us
    pallas_call x1, Pallas kernels, student(): pl.pallas_call(lambda *refs: student_kernel(parts, *refs), out_shape=jax....  6.84 us
    ppermute x3, starting transfers between devices, exchange(): return lax.ppermute(value, axis, [(k, k ^ stride) for k in range(size)])  3.22 us
    ppermute x3, waiting for transfers between devices, exchange(): return lax.ppermute(value, axis, [(k, k ^ stride) for k in range(size)])  1.26 us
    squeeze x1, local copies, waits for them, and re-layouts, compute(): piece = lax.dynamic_index_in_dim(grads, (mine + s) % dp, 0, False)  1 us
    convert_element_type x3, other arithmetic, compute(): moved = exchange(total.astype(BF16), axis, size, stride)  1 us
  transfers between devices with their start and end apart: 9, of which 5 were waited for; matrix products, arithmetic and copies ran while one was open for 2% of the time, Pallas kernels for 20%

profile of v2, /device:TPU:0, one launch (start us, length us, event | category | flops | bytes accessed | tf_op | source)
XLA Modules:
  0.0 43.8 jit_solution(7746795240899413257)
XLA Ops:
  0.7 6.8 %student.1 = bf16[4,48,896]{2,1,0:T(8,128)(2,1)} custom-call(bf16[128,1792]{1,0:T(8,128)(2,1)} %bitcast.15, bf16[128,896]{1,0:T(8,128)(2,1)} %refs_1_.1, bf16[128,1792]{1,0:T(8,128)(2,1)} %bitcast.16, bf16[128,3584]{1,0:T(8,128)(2,1)} %bitcast.14, bf16[8,3584]{1,0:T(8,128)(2,1)} %refs_4_.1, bf16[8,1792]{1,0:T(8,128)(2,1)} %refs_5_.5), custom_call_target="tpu_custom_call" | custom-call | tf_op jit(solution)/shard_map/student/pallas_call | solution.py:108
  7.5 1.0 %dynamic-slice_bitcast_fusion.2 = (bf16[48,896]{1,0:T(8,128)(2,1)S(1)}, bf16[48,896]{1,0:T(8,128)(2,1)S(1)}, bf16[48,896]{1,0:T(8,128)(2,1)S(1)}) fusion(bf16[4,48,896]{2,1,0:T(8,128)(2,1)} %student.1, s32[]{:T(128)S(6)} %select_n.30, s32[]{:T(128)S(6)} %select_n.34, s32[]{:T(128)S(6)} %select_n.32), kind=kLoop, calls=%fused_computation.9 | loop fusion | bytes 516108 | tf_op jit(solution)/shard_map/jit(dynamic_index_in_dim)/squeeze | solution.py:195
  8.5 5.1 %collective-permute-start.5 = (bf16[48,896]{1,0:T(8,128)(2,1)S(1)}, bf16[48,896]{1,0:T(8,128)(2,1)S(1)}, u32[]{:S(2)}, u32[]{:S(2)}) collective-permute-start(bf16[48,896]{1,0:T(8,128)(2,1)S(1)} %get-tuple-element.7), channel_id=1, source_target_pairs={{0,6},{2,0},{4,2},{6,4},{1,7},{3,1},{5,3},{7,5},{8,14},{10,8},{12,... | collective-permute-start | bytes 258056 | tf_op jit(solution)/shard_map/ppermute | solution.py:169
  13.7 0.0 collective-permute-start.4
  13.7 1.0 %collective-permute-start.3 = (bf16[48,896]{1,0:T(8,128)(2,1)S(1)}, bf16[48,896]{1,0:T(8,128)(2,1)S(1)}, u32[]{:S(2)}, u32[]{:S(2)}) collective-permute-start(bf16[48,896]{1,0:T(8,128)(2,1)S(1)} %get-tuple-element.6), channel_id=1, source_target_pairs={{0,2},{2,4},{4,6},{6,0},{1,3},{3,5},{5,7},{7,1},{8,10},{10,12},{12... | collective-permute-start | bytes 258056 | tf_op jit(solution)/shard_map/ppermute | solution.py:169
  14.7 0.0 copy-start
  14.7 0.0 copy-start.1
  14.7 1.9 %collective-permute-done.5 = bf16[48,896]{1,0:T(8,128)(2,1)S(1)} collective-permute-done((bf16[48,896]{1,0:T(8,128)(2,1)S(1)}, bf16[48,896]{1,0:T(8,128)(2,1)S(1)}, u32[]{:S(2)}, u32[]{:S(2)}) %collective-permute-start.5) | collective-permute-done | bytes 86048 | tf_op jit(solution)/shard_map/ppermute | solution.py:169
  16.6 4.9 %collective-permute-done.4 = bf16[48,896]{1,0:T(8,128)(2,1)S(1)} collective-permute-done((bf16[48,896]{1,0:T(8,128)(2,1)S(1)}, bf16[48,896]{1,0:T(8,128)(2,1)S(1)}, u32[]{:S(2)}, u32[]{:S(2)}) %collective-permute-start.4) | collective-permute-done | bytes 86048 | tf_op jit(solution)/shard_map/ppermute | solution.py:169
  21.5 0.0 collective-permute-done.3
  21.5 0.9 %fusion.4 = (bf16[48,896]{1,0:T(8,128)(2,1)S(1)}, f32[48,896]{1,0:T(8,128)S(1)}) fusion(bf16[48,896]{1,0:T(8,128)(2,1)S(1)} %collective-permute-done.5, bf16[48,896]{1,0:T(8,128)(2,1)S(1)} %collective-permute-done.4, bf16[48,896]{1,0:T(8,128)(2,1)S(1)} %collective-permute-done.3, bf16[4,48,896]{2,1,0:T(8,128)(2,1)} %student.1, s32[]{:T(128)S(6)} %select_n.28), kind=kLoop, calls=%fused_computation.13 | loop fusion | flops 344064 | bytes 602116 | tf_op jit(solution)/shard_map/convert_element_type | solution.py:207
  22.4 0.0 copy-start.5
  22.4 1.6 %collective-permute-start.6 = (bf16[48,896]{1,0:T(8,128)(2,1)S(1)}, bf16[48,896]{1,0:T(8,128)(2,1)S(1)}, u32[]{:S(2)}, u32[]{:S(2)}) collective-permute-start(bf16[48,896]{1,0:T(8,128)(2,1)S(1)} %get-tuple-element.4), channel_id=1, source_target_pairs={{0,1},{1,0},{2,3},{3,2},{4,5},{5,4},{6,7},{7,6},{8,9},{9,8},{10,11... | collective-permute-start | bytes 258056 | tf_op jit(solution)/shard_map/ppermute | solution.py:173
  24.0 0.0 copy-done.5
  24.0 0.6 %collective-permute-start = (s32[1,256]{1,0:T(1,128)S(1)}, s32[1,256]{1,0:T(1,128)S(1)}, u32[]{:S(2)}, u32[]{:S(2)}) collective-permute-start(s32[1,256]{1,0:T(1,128)S(1)} %copy-done.5), channel_id=1, source_target_pairs={{0,1},{1,0},{2,3},{3,2},{4,5},{5,4},{6,7},{7,6},{8,9},{9,8},{10,11... | collective-permute-start | bytes 3080 | tf_op jit(solution)/shard_map/ppermute | solution.py:169
  24.6 0.0 copy-done
  24.6 1.4 %collective-permute-start.1 = (bf16[1,256,256]{2,1,0:T(8,128)(2,1)S(1)}, bf16[1,256,256]{2,1,0:T(8,128)(2,1)S(1)}, u32[]{:S(2)}, u32[]{:S(2)}) collective-permute-start(bf16[1,256,256]{2,1,0:T(8,128)(2,1)S(1)} %copy-done), channel_id=1, source_target_pairs={{0,1},{1,0},{2,3},{3,2},{4,5},{5,4},{6,7},{7,6},{8,9},{9,8},{10,11... | collective-permute-start | bytes 393224 | tf_op jit(solution)/shard_map/ppermute | solution.py:169
  26.1 0.0 copy-done.1
  26.1 0.6 %collective-permute-start.2 = (bf16[1,256,256]{2,1,0:T(8,128)(2,1)S(1)}, bf16[1,256,256]{2,1,0:T(8,128)(2,1)S(1)}, u32[]{:S(2)}, u32[]{:S(2)}) collective-permute-start(bf16[1,256,256]{2,1,0:T(8,128)(2,1)S(1)} %copy-done.1), channel_id=1, source_target_pairs={{0,1},{1,0},{2,3},{3,2},{4,5},{5,4},{6,7},{7,6},{8,9},{9,8},{10,11... | collective-permute-start | bytes 393224 | tf_op jit(solution)/shard_map/ppermute | solution.py:169
  26.7 0.8 %copy.16.refs_0_ = s32[256,1]{1,0:T(8,128)} copy(s32[256,1]{0,1:T(1,128)S(1)} %bitcast.17) | data formatting | bytes 2048 | tf_op jit(solution)/shard_map/reshape | solution.py:189
  27.5 0.0 collective-permute-done.6
  27.5 0.1 collective-permute-start.7
  27.6 1.3 %collective-permute-done.7 = bf16[48,896]{1,0:T(8,128)(2,1)S(1)} collective-permute-done((bf16[48,896]{1,0:T(8,128)(2,1)S(1)}, bf16[48,896]{1,0:T(8,128)(2,1)S(1)}, u32[]{:S(2)}, u32[]{:S(2)}) %collective-permute-start.7) | collective-permute-done | bytes 86048 | tf_op jit(solution)/shard_map/ppermute | solution.py:173
  28.9 1.6 %collective-permute-start.8 = (bf16[48,896]{1,0:T(8,128)(2,1)S(1)}, bf16[48,896]{1,0:T(8,128)(2,1)S(1)}, u32[]{:S(2)}, u32[]{:S(2)}) collective-permute-start(bf16[48,896]{1,0:T(8,128)(2,1)S(1)} %fusion.3), channel_id=1, source_target_pairs={{0,16},{8,24},{16,0},{24,8},{1,17},{9,25},{17,1},{25,9},{2,18},{10... | collective-permute-start | bytes 258056 | tf_op jit(solution)/shard_map/ppermute | solution.py:173
  30.5 0.0 collective-permute-done
  30.5 0.0 copy-start.4
  30.5 0.5 %collective-permute-done.1.refs_4_ = bf16[1,256,256]{2,1,0:T(8,128)(2,1)S(1)} collective-permute-done((bf16[1,256,256]{2,1,0:T(8,128)(2,1)S(1)}, bf16[1,256,256]{2,1,0:T(8,128)(2,1)S(1)}, u32[]{:S(2)}, u32[]{:S(2)}) %collective-permute-start.1) | collective-permute-done | bytes 131104 | tf_op jit(solution)/shard_map/ppermute | solution.py:169
  31.0 0.0 copy-start.2
  31.0 1.6 %collective-permute-done.2.refs_6_ = bf16[1,256,256]{2,1,0:T(8,128)(2,1)S(1)} collective-permute-done((bf16[1,256,256]{2,1,0:T(8,128)(2,1)S(1)}, bf16[1,256,256]{2,1,0:T(8,128)(2,1)S(1)}, u32[]{:S(2)}, u32[]{:S(2)}) %collective-permute-start.2) | collective-permute-done | bytes 131104 | tf_op jit(solution)/shard_map/ppermute | solution.py:169
  32.6 0.0 copy-done.4
  32.6 0.0 copy-done.2
  32.6 0.0 copy-start.3
  32.6 0.7 %copy-done.3 = bf16[1,256,256]{2,1,0:T(8,128)(2,1)} copy-done((bf16[1,256,256]{2,1,0:T(8,128)(2,1)}, bf16[1,256,256]{2,1,0:T(8,128)(2,1)S(1)}, u32[]{:S(2)}) %copy-start.3) | copy-done | bytes 131096
  33.3 4.3 %shard_map.129.refs_7_ = bf16[1,256,1792]{2,1,0:T(8,128)(2,1)} custom-call(s32[256,1]{1,0:T(8,128)} %copy.16.refs_0_, s32[1,512]{1,0:T(1,128)} %copy-done.4, bf16[1,256,1792]{2,1,0:T(8,128)(2,1)} %refs_2_.3, bf16[1,256,256]{2,1,0:T(8,128)(2,1)} %refs_3_.3, bf16[1,256,256]{2,1,0:T(8,128)(2,1)} %copy-done.2, bf16[1,256,256]{2,1,0:T(8,128)(2,1)} %refs_5_.4, ...), custom_call_target="tpu_custom_call" | custom-call | tf_op jit(solution)/shard_map/pallas_call | solution.py:157
  37.6 4.3 %shard_map.130 = bf16[1,256,1792]{2,1,0:T(8,128)(2,1)} custom-call(s32[256,1]{1,0:T(8,128)} %copy.16.refs_0_, s32[1,512]{1,0:T(1,128)} %copy-done.4, bf16[1,256,1792]{2,1,0:T(8,128)(2,1)} %refs_2_.3, bf16[1,256,256]{2,1,0:T(8,128)(2,1)} %refs_3_.3, bf16[1,256,256]{2,1,0:T(8,128)(2,1)} %copy-done.2, ...), custom_call_target="tpu_custom_call", output_to_operand_aliasing={{}: (7, {})} | custom-call | tf_op jit(solution)/shard_map/pallas_call | solution.py:157
  41.9 0.0 collective-permute-done.8
  41.9 0.7 %slice.12 = f32[32,896]{1,0:T(8,128)} slice(f32[48,896]{1,0:T(8,128)S(1)} %convert_add_fusion.1), slice={[16:48], [0:896]} | slice | bytes 229376 | tf_op jit(solution)/shard_map/slice | solution.py:213
  42.6 0.6 %slice.13 = f32[8,896]{1,0:T(8,128)} slice(f32[48,896]{1,0:T(8,128)S(1)} %convert_add_fusion.1), slice={[0:8], [0:896]} | slice | bytes 57344 | tf_op jit(solution)/shard_map/slice | solution.py:211
  43.2 0.6 %slice.14 = f32[8,448]{1,0:T(8,128)} slice(f32[48,896]{1,0:T(8,128)S(1)} %convert_add_fusion.1), slice={[8:16], [0:448]} | slice | bytes 28672 | tf_op jit(solution)/shard_map/slice | solution.py:212
  (5 shorter events, 0.1 us)
Async XLA Ops:
  8.5 8.0 %collective-permute-start.5 = (bf16[48,896]{1,0:T(8,128)(2,1)S(1)}, bf16[48,896]{1,0:T(8,128)(2,1)S(1)}, u32[]{:S(2)}, u32[]{:S(2)}) collective-permute-start(bf16[48,896]{1,0:T(8,128)(2,1)S(1)} %get-tuple-element.7), channel_id=1, source_target_pairs={{0,6},{2,0},{4,2},{6,4},{1,7},{3,1},{5,3},{7,5},{8,14},{10,8},{12,... | collective-permute-start | bytes 258056 | tf_op jit(solution)/shard_map/ppermute | solution.py:169
  13.7 7.8 %collective-permute-start.4 = (bf16[48,896]{1,0:T(8,128)(2,1)S(1)}, bf16[48,896]{1,0:T(8,128)(2,1)S(1)}, u32[]{:S(2)}, u32[]{:S(2)}) collective-permute-start(bf16[48,896]{1,0:T(8,128)(2,1)S(1)} %get-tuple-element.8), channel_id=1, source_target_pairs={{0,4},{2,6},{4,0},{6,2},{1,5},{3,7},{5,1},{7,3},{8,12},{10,14},{12... | collective-permute-start | bytes 258056 | tf_op jit(solution)/shard_map/ppermute | solution.py:169
  13.7 7.8 %collective-permute-start.3 = (bf16[48,896]{1,0:T(8,128)(2,1)S(1)}, bf16[48,896]{1,0:T(8,128)(2,1)S(1)}, u32[]{:S(2)}, u32[]{:S(2)}) collective-permute-start(bf16[48,896]{1,0:T(8,128)(2,1)S(1)} %get-tuple-element.6), channel_id=1, source_target_pairs={{0,2},{2,4},{4,6},{6,0},{1,3},{3,5},{5,7},{7,1},{8,10},{10,12},{12... | collective-permute-start | bytes 258056 | tf_op jit(solution)/shard_map/ppermute | solution.py:169
  14.7 10.0 %copy-start = (bf16[1,256,256]{2,1,0:T(8,128)(2,1)S(1)}, bf16[1,256,256]{2,1,0:T(8,128)(2,1)}, u32[]{:S(2)}) copy-start(bf16[1,256,256]{2,1,0:T(8,128)(2,1)} %refs_3_.3) | copy-start | bytes 393220
  14.7 11.4 %copy-start.1 = (bf16[1,256,256]{2,1,0:T(8,128)(2,1)S(1)}, bf16[1,256,256]{2,1,0:T(8,128)(2,1)}, u32[]{:S(2)}) copy-start(bf16[1,256,256]{2,1,0:T(8,128)(2,1)} %refs_5_.4) | copy-start | bytes 393220
  22.4 1.6 %copy-start.5 = (s32[1,256]{1,0:T(1,128)S(1)}, s32[1,256]{1,0:T(1,128)}, u32[]{:S(2)}) copy-start(s32[1,256]{1,0:T(1,128)} %param.19) | copy-start | bytes 3076
  22.4 5.0 %collective-permute-start.6 = (bf16[48,896]{1,0:T(8,128)(2,1)S(1)}, bf16[48,896]{1,0:T(8,128)(2,1)S(1)}, u32[]{:S(2)}, u32[]{:S(2)}) collective-permute-start(bf16[48,896]{1,0:T(8,128)(2,1)S(1)} %get-tuple-element.4), channel_id=1, source_target_pairs={{0,1},{1,0},{2,3},{3,2},{4,5},{5,4},{6,7},{7,6},{8,9},{9,8},{10,11... | collective-permute-start | bytes 258056 | tf_op jit(solution)/shard_map/ppermute | solution.py:173
  24.0 6.4 %collective-permute-start = (s32[1,256]{1,0:T(1,128)S(1)}, s32[1,256]{1,0:T(1,128)S(1)}, u32[]{:S(2)}, u32[]{:S(2)}) collective-permute-start(s32[1,256]{1,0:T(1,128)S(1)} %copy-done.5), channel_id=1, source_target_pairs={{0,1},{1,0},{2,3},{3,2},{4,5},{5,4},{6,7},{7,6},{8,9},{9,8},{10,11... | collective-permute-start | bytes 3080 | tf_op jit(solution)/shard_map/ppermute | solution.py:169
  24.6 6.4 %collective-permute-start.1 = (bf16[1,256,256]{2,1,0:T(8,128)(2,1)S(1)}, bf16[1,256,256]{2,1,0:T(8,128)(2,1)S(1)}, u32[]{:S(2)}, u32[]{:S(2)}) collective-permute-start(bf16[1,256,256]{2,1,0:T(8,128)(2,1)S(1)} %copy-done), channel_id=1, source_target_pairs={{0,1},{1,0},{2,3},{3,2},{4,5},{5,4},{6,7},{7,6},{8,9},{9,8},{10,11... | collective-permute-start | bytes 393224 | tf_op jit(solution)/shard_map/ppermute | solution.py:169
  26.1 6.6 %collective-permute-start.2 = (bf16[1,256,256]{2,1,0:T(8,128)(2,1)S(1)}, bf16[1,256,256]{2,1,0:T(8,128)(2,1)S(1)}, u32[]{:S(2)}, u32[]{:S(2)}) collective-permute-start(bf16[1,256,256]{2,1,0:T(8,128)(2,1)S(1)} %copy-done.1), channel_id=1, source_target_pairs={{0,1},{1,0},{2,3},{3,2},{4,5},{5,4},{6,7},{7,6},{8,9},{9,8},{10,11... | collective-permute-start | bytes 393224 | tf_op jit(solution)/shard_map/ppermute | solution.py:169
  27.5 1.3 %collective-permute-start.7 = (bf16[48,896]{1,0:T(8,128)(2,1)S(1)}, bf16[48,896]{1,0:T(8,128)(2,1)S(1)}, u32[]{:S(2)}, u32[]{:S(2)}) collective-permute-start(bf16[48,896]{1,0:T(8,128)(2,1)S(1)} %fusion.2), channel_id=1, source_target_pairs={{0,8},{8,0},{16,24},{24,16},{1,9},{9,1},{17,25},{25,17},{2,10},{10... | collective-permute-start | bytes 258056 | tf_op jit(solution)/shard_map/ppermute | solution.py:173
  28.9 13.0 %collective-permute-start.8 = (bf16[48,896]{1,0:T(8,128)(2,1)S(1)}, bf16[48,896]{1,0:T(8,128)(2,1)S(1)}, u32[]{:S(2)}, u32[]{:S(2)}) collective-permute-start(bf16[48,896]{1,0:T(8,128)(2,1)S(1)} %fusion.3), channel_id=1, source_target_pairs={{0,16},{8,24},{16,0},{24,8},{1,17},{9,25},{17,1},{25,9},{2,18},{10... | collective-permute-start | bytes 258056 | tf_op jit(solution)/shard_map/ppermute | solution.py:173
  30.5 2.2 %copy-start.4 = (s32[1,512]{1,0:T(1,128)}, s32[1,512]{1,0:T(1,128)S(1)}, u32[]{:S(2)}) copy-start(s32[1,512]{1,0:T(1,128)S(1)} %constant_dynamic-update-slice_fusion.refs_1_) | copy-start | bytes 6148
  31.0 1.6 %copy-start.2 = (bf16[1,256,256]{2,1,0:T(8,128)(2,1)}, bf16[1,256,256]{2,1,0:T(8,128)(2,1)S(1)}, u32[]{:S(2)}) copy-start(bf16[1,256,256]{2,1,0:T(8,128)(2,1)S(1)} %collective-permute-done.1.refs_4_) | copy-start | bytes 393220
  32.6 0.7 %copy-start.3 = (bf16[1,256,256]{2,1,0:T(8,128)(2,1)}, bf16[1,256,256]{2,1,0:T(8,128)(2,1)S(1)}, u32[]{:S(2)}) copy-start(bf16[1,256,256]{2,1,0:T(8,128)(2,1)S(1)} %collective-permute-done.2.refs_6_) | copy-start | bytes 393220
